TPU v7x, 32 devices: a whole 2x2x4 slice. The times are simulated.
32 devices in a mesh: group: 4 (over y, x), dp: 2 (over core), tensor: 4 (over z).
Axes of the slice: x: 2, y: 2, z: 4, core: 2. Of those that a mesh axis runs over, the one named last changes fastest.
Arguments:
- tokens: bfloat16 [8192, 2048], P(('group', 'dp')), may hold values from -6 to 6
- norm_gain: bfloat16 [2048], replicated, may hold values from 0.099609375 to 1.8984375
- w_query: bfloat16 [2048, 2048], P(None, 'tensor'), may hold values from -0.25 to 0.25
- w_keyval: bfloat16 [2048, 512], P(None, 'tensor'), may hold values from -0.125 to 0.125
- w_out: bfloat16 [2048, 2048], P('tensor'), may hold values from -0.8984375 to 0.8984375
- kv_cache: bfloat16 [4, 32, 16, 128, 512], P(None, ('group', 'dp'), None, None, 'tensor'), may hold values from -400 to 400
- lengths: int32 [32, 2], P(('group', 'dp')), may hold values from 0 to 2048, as said below
- dest_slot: int32 [32, 16], replicated, may hold values from 0 to 511, as said below
Outputs:
- mixed: bfloat16 [8192, 2048], P(('group', 'dp', 'tensor'))
- decode_cache: bfloat16 [4, 512, 128, 512], P(None, ('group', 'dp'), None, 'tensor')
Inputs may be any that keep to these rules, and one draw needn't show every extreme that they name: lengths[p, 0] lies in 0 to 2048 and lengths[p, 1] in 1 to 256; 2048 and 256 are each taken by some prompt; the prompts r * 4 to r * 4 + 3 of each index r of group and dp together hold exactly 32 live blocks. dest_slot is a permutation of the 512 slots; the slots of the index r of group and dp together are r * 4 * 16 onward; the blocks of prompts r * 4 to r * 4 + 3 send exactly 8 blocks to each index, of which exactly 4 is live.
All inputs are finite; a program needn't handle non-finite values.
Results may differ from a plain program's by a relative error of at most 0.009.
Values may be sent and summed in bfloat16 or wider, within the bound.
A program may use at most 128 MiB of HBM per device.

v0:
```python
import jax
import jax.numpy as jnp
from jax import lax
from jax.sharding import PartitionSpec as P

HD = 64


def per_device(tokens, norm_gain, w_query, w_keyval, w_out, kv_cache, lengths, dest_slot):
    tok_rows = tokens.shape[0]
    prompts = lengths.shape[0]
    fresh_rows = tok_rows // prompts
    heads_local = w_query.shape[1] // HD
    kv_local = w_keyval.shape[1] // (2 * HD)
    group_size = heads_local // kv_local
    layers = kv_cache.shape[0]
    blocks_win = kv_cache.shape[2]
    block_len = kv_cache.shape[3]
    lane_width = kv_cache.shape[4]
    window = blocks_win * block_len
    tokens_f = tokens.astype(jnp.float32)
    normed = (
        tokens_f
        * lax.rsqrt(jnp.mean(tokens_f * tokens_f, axis=-1, keepdims=True) + 1e-05)
        * norm_gain.astype(jnp.float32)
    ).astype(jnp.bfloat16)
    query = jnp.dot(normed, w_query, preferred_element_type=jnp.float32).astype(jnp.bfloat16)
    query = query.reshape(prompts, fresh_rows, kv_local, group_size, HD)
    keyval = jnp.dot(normed, w_keyval, preferred_element_type=jnp.float32).astype(jnp.bfloat16)
    keyval = keyval.reshape(prompts, fresh_rows, kv_local, 2, HD)
    cache = kv_cache[0].reshape(prompts, window, kv_local, 2, HD)
    scale = 1.0 / HD**0.5
    query_pos = jnp.arange(fresh_rows)[:, None]
    key_pos = jnp.arange(window + fresh_rows)[None, :]

    def attend(items):
        query_p, cache_p, fresh_p, history, fresh_len = items
        pairs = jnp.concatenate([cache_p, fresh_p], axis=0)
        scores = (
            jnp.einsum(
                "ckgd,tkd->kgct", query_p, pairs[:, :, 0], preferred_element_type=jnp.float32
            )
            * scale
        )
        visible = jnp.where(
            key_pos < window,
            (key_pos >= window - history) & (key_pos >= query_pos + 1),
            key_pos - window <= query_pos,
        )
        scores = jnp.where(visible, scores, -1e30)
        scores = scores - jnp.max(scores, axis=-1, keepdims=True)
        expo = jnp.exp(scores)
        weights = (expo / jnp.sum(expo, axis=-1, keepdims=True)).astype(jnp.bfloat16)
        mixed_p = jnp.einsum(
            "kgct,tkd->ckgd", weights, pairs[:, :, 1], preferred_element_type=jnp.float32
        )
        mixed_p = mixed_p.astype(jnp.bfloat16).reshape(fresh_rows, heads_local * HD)
        return jnp.where(
            (jnp.arange(fresh_rows) < fresh_len)[:, None], mixed_p, jnp.zeros_like(mixed_p)
        )

    attn = lax.map(attend, (query, cache, keyval, lengths[:, 0], lengths[:, 1]))
    attn = attn.reshape(tok_rows, heads_local * HD)
    mixed = lax.psum_scatter(
        jnp.dot(attn, w_out, preferred_element_type=jnp.float32),
        "tensor",
        scatter_dimension=0,
        tiled=True,
    ).astype(jnp.bfloat16)
    per_dev = prompts * blocks_win
    devices = lax.axis_size(("group", "dp"))
    per_peer = per_dev // devices
    my_index = lax.axis_index(("group", "dp"))
    dest_all = dest_slot.reshape(devices, per_dev)
    recv_all = dest_all // per_dev
    same_dest = recv_all[:, :, None] == recv_all[:, None, :]
    earlier = jnp.arange(per_dev)[None, :] < jnp.arange(per_dev)[:, None]
    own_recv = lax.dynamic_index_in_dim(recv_all, my_index, 0, keepdims=False)
    senders = jnp.arange(devices, dtype=jnp.int32)[:, None]
    capacity = per_peer // 2
    lengths_every = lax.all_gather(lengths, ("group", "dp"), axis=0, tiled=True)
    live_all = (
        (jnp.arange(blocks_win)[None, :] + 1) * block_len > window - lengths_every[:, 0:1]
    ).reshape(devices, per_dev)
    live_rank = jnp.sum(same_dest & earlier[None, :, :] & live_all[:, None, :], axis=2)
    own_live = lax.dynamic_index_in_dim(live_all, my_index, 0, keepdims=False)
    own_live_rank = lax.dynamic_index_in_dim(live_rank, my_index, 0, keepdims=False)
    send_pos = jnp.where(own_live, own_recv * capacity + own_live_rank, devices * capacity)
    send_idx = (
        jnp.zeros((devices * capacity,), jnp.int32)
        .at[send_pos]
        .set(jnp.arange(per_dev, dtype=jnp.int32), mode="drop")
    )
    raw_blocks = kv_cache.reshape(layers, per_dev, block_len, lane_width)
    outgoing = jnp.take(raw_blocks, send_idx, axis=1)
    incoming = lax.all_to_all(outgoing, ("group", "dp"), split_axis=1, concat_axis=1, tiled=True)
    where_from = senders * capacity + live_rank
    valid = (recv_all == my_index) & live_all
    slot_local = jnp.where(valid, dest_all - my_index * per_dev, per_dev)
    source_idx = (
        jnp.full((per_dev,), devices * capacity, jnp.int32)
        .at[slot_local.reshape(-1)]
        .set(where_from.reshape(-1), mode="drop")
    )
    decode_cache = jnp.take(incoming, source_idx, axis=1, mode="fill", fill_value=0)
    return (mixed, decode_cache)


def solution(mesh):
    in_specs = (
        P(("group", "dp"), None),
        P(),
        P(None, "tensor"),
        P(None, "tensor"),
        P("tensor", None),
        P(None, ("group", "dp"), None, None, "tensor"),
        P(("group", "dp"), None),
        P(),
    )
    out_specs = (P(("group", "dp", "tensor"), None), P(None, ("group", "dp"), None, "tensor"))
    return jax.shard_map(
        per_device, mesh=mesh, in_specs=in_specs, out_specs=out_specs, check_vma=False
    )
```

profile of v0, /device:TPU:0, one launch (start us, length us, event | category | flops | bytes accessed | tf_op | source)
XLA Modules:
  0.0 344.5 jit_solution(16174500329635103676)
XLA Ops:
  27.7 5.3 %convolution_convert_fusion = bf16[1024,512]{1,0:T(8,128)(2,1)S(1)} fusion(bf16[2048,512]{1,0:T(8,128)(2,1)} %param.12, bf16[1024,2048]{1,0:T(8,128)(2,1)} %param.10, f32[2048]{0:T(1024)S(1)} %convert_element_type.40, f32[1024]{0:T(1024)S(1)} %add_rsqrt_fusion), kind=kOutput, calls=%fused_computation.49 | convolution fusion | flops 2156396544 | bytes 7352320 | tf_op jit(solution)/shard_map/dot_general | solution.py:27
  38.1 142.6 %while.14 = (s32[]{:T(128)}, bf16[4,256,512]{2,1,0:T(8,128)(2,1)}, s32[4]{0:T(128)}, bf16[4,2048,1,2,64]{1,4,3,2,0:T(8,128)(2,1)}, bf16[4,256,1,2,64]{1,4,3,2,0:...) while((s32[]{:T(128)}, bf16[4,256,512]{2,1,0:T(8,128)(2,1)}, ...), condition=%wide.region_4.5_spmd.clone.clone, body=%wide.region_1.4_spmd.clone.clone.sunk | while | flops 1268387072 | bytes 63510268 | solution.py:62
  43.3 9.0 %fusion.59 = (f32[8,256]{1,0:T(8,128)S(1)}, f32[2304,256,8]{1,0,2:T(8,128)}) fusion(pred[256,2304]{0,1:T(8,128)(4,1)S(1)} %fusion.58, bf16[4,256,1,8,64]{1,4,3,2,0:T(8,128)(2,1)} %get-tuple-element.310, s32[]{:T(128)S(6)} %copy.74, bf16[256,1,2,64]{0,3,2,1:T(8,128)(2,1)S(1)} %dynamic-slice_bitcast_fusion.4, ...), kind=kOutput, calls=%fused_computation.10.clone.1 | convolution fusion | flops 618723328 | bytes 20324356 | tf_op jit(solution)/shard_map/while/body/eval_jaxpr/ckgd,tkd->kgct/dot_general | solution.py:40
  52.3 10.2 %fusion.60 = f32[8,256]{1,0:T(8,128)S(1)} fusion(f32[2304,256,8]{1,0,2:T(8,128)} %get-tuple-element.284, f32[8,256]{1,0:T(8,128)S(1)} %get-tuple-element.285, pred[256,2304]{0,1:T(8,128)(4,1)S(1)} %fusion.58), kind=kLoop, calls=%fused_computation.9.clone.1 | loop fusion | flops 18872320 | bytes 19480576 | tf_op jit(solution)/shard_map/while/body/eval_jaxpr/reduce_sum | solution.py:53
  62.5 9.0 %fusion.61 = bf16[64,8,256]{2,0,1:T(8,128)(2,1)S(1)} fusion(f32[8,256]{1,0:T(8,128)S(1)} %fusion.60, f32[8,256]{1,0:T(8,128)S(1)} %get-tuple-element.285, f32[2304,256,8]{1,0,2:T(8,128)} %get-tuple-element.284, pred[256,2304]{0,1:T(8,128)(4,1)S(1)} %fusion.58, bf16[2048,1,2,64]{0,3,2,1:T(8,128)(2,1)S(1)} %dynamic-slice_bitcast_fusion.5, ...), kind=kOutput, calls=%fused_computation.17.clone.1 | convolution fusion | flops 628293632 | bytes 20332544 | tf_op jit(solution)/shard_map/while/body/eval_jaxpr/kgct,tkd->ckgd/dot_general | solution.py:54
  78.9 9.0 %fusion.59 = (f32[8,256]{1,0:T(8,128)S(1)}, f32[2304,256,8]{1,0,2:T(8,128)}) fusion(pred[256,2304]{0,1:T(8,128)(4,1)S(1)} %fusion.58, bf16[4,256,1,8,64]{1,4,3,2,0:T(8,128)(2,1)} %get-tuple-element.310, s32[]{:T(128)S(6)} %copy.74, bf16[256,1,2,64]{0,3,2,1:T(8,128)(2,1)S(1)} %dynamic-slice_bitcast_fusion.4, ...), kind=kOutput, calls=%fused_computation.10.clone.1 | convolution fusion | flops 618723328 | bytes 20324356 | tf_op jit(solution)/shard_map/while/body/eval_jaxpr/ckgd,tkd->kgct/dot_general | solution.py:40
  87.9 10.2 %fusion.60 = f32[8,256]{1,0:T(8,128)S(1)} fusion(f32[2304,256,8]{1,0,2:T(8,128)} %get-tuple-element.284, f32[8,256]{1,0:T(8,128)S(1)} %get-tuple-element.285, pred[256,2304]{0,1:T(8,128)(4,1)S(1)} %fusion.58), kind=kLoop, calls=%fused_computation.9.clone.1 | loop fusion | flops 18872320 | bytes 19480576 | tf_op jit(solution)/shard_map/while/body/eval_jaxpr/reduce_sum | solution.py:53
  98.1 9.0 %fusion.61 = bf16[64,8,256]{2,0,1:T(8,128)(2,1)S(1)} fusion(f32[8,256]{1,0:T(8,128)S(1)} %fusion.60, f32[8,256]{1,0:T(8,128)S(1)} %get-tuple-element.285, f32[2304,256,8]{1,0,2:T(8,128)} %get-tuple-element.284, pred[256,2304]{0,1:T(8,128)(4,1)S(1)} %fusion.58, bf16[2048,1,2,64]{0,3,2,1:T(8,128)(2,1)S(1)} %dynamic-slice_bitcast_fusion.5, ...), kind=kOutput, calls=%fused_computation.17.clone.1 | convolution fusion | flops 628293632 | bytes 20332544 | tf_op jit(solution)/shard_map/while/body/eval_jaxpr/kgct,tkd->ckgd/dot_general | solution.py:54
  114.6 9.0 %fusion.59 = (f32[8,256]{1,0:T(8,128)S(1)}, f32[2304,256,8]{1,0,2:T(8,128)}) fusion(pred[256,2304]{0,1:T(8,128)(4,1)S(1)} %fusion.58, bf16[4,256,1,8,64]{1,4,3,2,0:T(8,128)(2,1)} %get-tuple-element.310, s32[]{:T(128)S(6)} %copy.74, bf16[256,1,2,64]{0,3,2,1:T(8,128)(2,1)S(1)} %dynamic-slice_bitcast_fusion.4, ...), kind=kOutput, calls=%fused_computation.10.clone.1 | convolution fusion | flops 618723328 | bytes 20324356 | tf_op jit(solution)/shard_map/while/body/eval_jaxpr/ckgd,tkd->kgct/dot_general | solution.py:40
  123.6 10.2 %fusion.60 = f32[8,256]{1,0:T(8,128)S(1)} fusion(f32[2304,256,8]{1,0,2:T(8,128)} %get-tuple-element.284, f32[8,256]{1,0:T(8,128)S(1)} %get-tuple-element.285, pred[256,2304]{0,1:T(8,128)(4,1)S(1)} %fusion.58), kind=kLoop, calls=%fused_computation.9.clone.1 | loop fusion | flops 18872320 | bytes 19480576 | tf_op jit(solution)/shard_map/while/body/eval_jaxpr/reduce_sum | solution.py:53
  133.8 9.0 %fusion.61 = bf16[64,8,256]{2,0,1:T(8,128)(2,1)S(1)} fusion(f32[8,256]{1,0:T(8,128)S(1)} %fusion.60, f32[8,256]{1,0:T(8,128)S(1)} %get-tuple-element.285, f32[2304,256,8]{1,0,2:T(8,128)} %get-tuple-element.284, pred[256,2304]{0,1:T(8,128)(4,1)S(1)} %fusion.58, bf16[2048,1,2,64]{0,3,2,1:T(8,128)(2,1)S(1)} %dynamic-slice_bitcast_fusion.5, ...), kind=kOutput, calls=%fused_computation.17.clone.1 | convolution fusion | flops 628293632 | bytes 20332544 | tf_op jit(solution)/shard_map/while/body/eval_jaxpr/kgct,tkd->ckgd/dot_general | solution.py:54
  150.2 9.0 %fusion.59 = (f32[8,256]{1,0:T(8,128)S(1)}, f32[2304,256,8]{1,0,2:T(8,128)}) fusion(pred[256,2304]{0,1:T(8,128)(4,1)S(1)} %fusion.58, bf16[4,256,1,8,64]{1,4,3,2,0:T(8,128)(2,1)} %get-tuple-element.310, s32[]{:T(128)S(6)} %copy.74, bf16[256,1,2,64]{0,3,2,1:T(8,128)(2,1)S(1)} %dynamic-slice_bitcast_fusion.4, ...), kind=kOutput, calls=%fused_computation.10.clone.1 | convolution fusion | flops 618723328 | bytes 20324356 | tf_op jit(solution)/shard_map/while/body/eval_jaxpr/ckgd,tkd->kgct/dot_general | solution.py:40
  159.2 10.2 %fusion.60 = f32[8,256]{1,0:T(8,128)S(1)} fusion(f32[2304,256,8]{1,0,2:T(8,128)} %get-tuple-element.284, f32[8,256]{1,0:T(8,128)S(1)} %get-tuple-element.285, pred[256,2304]{0,1:T(8,128)(4,1)S(1)} %fusion.58), kind=kLoop, calls=%fused_computation.9.clone.1 | loop fusion | flops 18872320 | bytes 19480576 | tf_op jit(solution)/shard_map/while/body/eval_jaxpr/reduce_sum | solution.py:53
  169.4 9.0 %fusion.61 = bf16[64,8,256]{2,0,1:T(8,128)(2,1)S(1)} fusion(f32[8,256]{1,0:T(8,128)S(1)} %fusion.60, f32[8,256]{1,0:T(8,128)S(1)} %get-tuple-element.285, f32[2304,256,8]{1,0,2:T(8,128)} %get-tuple-element.284, pred[256,2304]{0,1:T(8,128)(4,1)S(1)} %fusion.58, bf16[2048,1,2,64]{0,3,2,1:T(8,128)(2,1)S(1)} %dynamic-slice_bitcast_fusion.5, ...), kind=kOutput, calls=%fused_computation.17.clone.1 | convolution fusion | flops 628293632 | bytes 20332544 | tf_op jit(solution)/shard_map/while/body/eval_jaxpr/kgct,tkd->ckgd/dot_general | solution.py:54
  180.8 6.8 %fusion.45 = f32[1024,2048]{1,0:T(8,128)} fusion(bf16[1024,512]{1,0:T(8,128)(2,1)} %bitcast.102, bf16[512,2048]{1,0:T(8,128)(2,1)S(1)} %copy-done), kind=kOutput, calls=%fused_computation.92 | convolution fusion | flops 2147483648 | bytes 11534336 | tf_op jit(solution)/shard_map/dot_general | solution.py:65
  187.8 10.3 %all-gather = s32[8,4,2]{1,2,0:T(2,128)S(1)} all-gather(s32[1,4,2]{1,2,0:T(2,128)S(1)} %bitcast.100), channel_id=1, replica_groups=mesh['group'=4,'dp'=2,'tensor'=4] {'group','dp'}, dimensions={0}, use_global_device_ids=true | all-gather | bytes 288 | tf_op jit(solution)/shard_map/all_gather | solution.py:81
  200.0 6.5 %gather_fusion = bf16[32,4,128,128]{3,2,1,0:T(8,128)(2,1)} fusion(bf16[4,64,128,128]{3,2,1,0:T(8,128)(2,1)} %bitcast.99, s32[1024]{0:T(1024)S(1)} %pad_clamp_fusion.1), kind=kCustom, calls=%fused_computation | custom fusion | bytes 8388736 | tf_op jit(solution)/shard_map/jit(_take)/gather | solution.py:95
  206.5 4.7 %select_bitcast_fusion.1 = bf16[4,32,128,128]{3,2,0,1:T(8,128)(2,1)} fusion(bf16[32,4,128,128]{3,2,1,0:T(8,128)(2,1)} %gather_fusion, pred[32]{0:T(512)(128)(4,1)S(1)} %compare_and_fusion), kind=kLoop, calls=%fused_computation.48 | loop fusion | flops 2097152 | bytes 8388640 | tf_op jit(solution)/shard_map/jit(_take)/select_n | solution.py:95
  218.7 46.2 %all-to-all-done = bf16[4,32,128,128]{3,2,0,1:T(8,128)(2,1)} async-done(((bf16[4,32,128,128]{3,2,0,1:T(8,128)(2,1)}), bf16[4,32,128,128]{3,2,0,1:T(8,128)(2,1)}, u32[]{:S(2)}, u32[]{:S(2)}) %all-to-all-start) | async-done | bytes 4194336 | tf_op jit(solution)/shard_map/all_to_all | solution.py:96
  264.9 4.7 %copy.60 = bf16[4,32,128,128]{3,2,1,0:T(8,128)(2,1)} copy(bf16[4,32,128,128]{3,2,0,1:T(8,128)(2,1)} %all-to-all-done) | data formatting | bytes 8388608 | tf_op jit(solution)/shard_map/all_to_all | solution.py:96
  269.6 7.8 %gather_fusion.1 = bf16[64,4,128,128]{3,2,1,0:T(8,128)(2,1)} fusion(bf16[4,32,128,128]{3,2,1,0:T(8,128)(2,1)} %copy.60, s32[1024]{0:T(1024)S(1)} %pad_clamp_fusion), kind=kCustom, calls=%fused_computation.1 | custom fusion | bytes 16777472 | tf_op jit(solution)/shard_map/jit(_take)/gather | solution.py:105
  277.4 7.3 %select_bitcast_fusion = bf16[4,64,128,128]{3,2,0,1:T(8,128)(2,1)} fusion(bf16[64,4,128,128]{3,2,1,0:T(8,128)(2,1)} %gather_fusion.1, pred[64]{0:T(512)(128)(4,1)S(1)} %compare_and_fusion.1), kind=kLoop, calls=%fused_computation.47 | loop fusion | flops 4194304 | bytes 16777280 | tf_op jit(solution)/shard_map/jit(_take)/select_n | solution.py:105
  284.7 10.5 %copy.61 = bf16[4,64,128,128]{3,2,1,0:T(8,128)(2,1)} copy(bf16[4,64,128,128]{3,2,0,1:T(8,128)(2,1)} %select_bitcast_fusion) | data formatting | bytes 16777216
  295.2 39.7 %reduce-scatter.2.cloned.1.call-done = f32[256,2048]{1,0:T(8,128)} async-done(((f32[1024,2048]{1,0:T(8,128)}), f32[256,2048]{1,0:T(8,128)}) %reduce-scatter.2.cloned.1.call-update) | async-done | bytes 2097168 | tf_op jit(solution)/shard_map/reduce_scatter | solution.py:64
  (114 shorter events, 64.6 us)
Async XLA Ops:
  7.2 173.6 %copy-start = (bf16[512,2048]{1,0:T(8,128)(2,1)S(1)}, bf16[512,2048]{1,0:T(8,128)(2,1)}, u32[]{:S(2)}) copy-start(bf16[512,2048]{1,0:T(8,128)(2,1)} %param.14) | copy-start | bytes 6291460
  7.2 13.2 %copy-start.2 = (bf16[2048]{0:T(1024)(128)(2,1)S(1)}, bf16[2048]{0:T(1024)(128)(2,1)}, u32[]{:S(2)}) copy-start(bf16[2048]{0:T(1024)(128)(2,1)} %param.11) | copy-start | bytes 12292
  7.2 327.7 %reduce-scatter.2.cloned.1.call-start = ((), (), s32[]{:S(2)}) async-start(), calls=%async_computation.2 | async-start | bytes 10485760 | tf_op jit(solution)/shard_map/reduce_scatter | solution.py:64
  62.4 9.1 %copy-start.4 = (s32[4]{0:T(128)S(1)}, s32[4]{0:T(128)}, u32[]{:S(2)}) copy-start(s32[4]{0:T(128)} %get-tuple-element.306) | copy-start | bytes 52 | tf_op jit(solution)/shard_map/while
  98.1 9.1 %copy-start.4 = (s32[4]{0:T(128)S(1)}, s32[4]{0:T(128)}, u32[]{:S(2)}) copy-start(s32[4]{0:T(128)} %get-tuple-element.306) | copy-start | bytes 52 | tf_op jit(solution)/shard_map/while
  133.8 9.1 %copy-start.4 = (s32[4]{0:T(128)S(1)}, s32[4]{0:T(128)}, u32[]{:S(2)}) copy-start(s32[4]{0:T(128)} %get-tuple-element.306) | copy-start | bytes 52 | tf_op jit(solution)/shard_map/while
  169.4 9.1 %copy-start.4 = (s32[4]{0:T(128)S(1)}, s32[4]{0:T(128)}, u32[]{:S(2)}) copy-start(s32[4]{0:T(128)} %get-tuple-element.306) | copy-start | bytes 52 | tf_op jit(solution)/shard_map/while
  180.8 6.8 %copy-start.1 = (s32[32,16]{0,1:T(8,128)S(1)}, s32[32,16]{0,1:T(8,128)}, u32[]{:S(2)}) copy-start(s32[32,16]{0,1:T(8,128)} %param.17) | copy-start | bytes 6148
  180.8 7.0 %copy-start.3 = (s32[4,2]{0,1:T(2,128)S(1)}, s32[4,2]{0,1:T(2,128)}, u32[]{:S(2)}) copy-start(s32[4,2]{0,1:T(2,128)} %param.16) | copy-start | bytes 100
  211.1 53.7 %all-to-all-start = ((bf16[4,32,128,128]{3,2,0,1:T(8,128)(2,1)}), bf16[4,32,128,128]{3,2,0,1:T(8,128)(2,1)}, u32[]{:S(2)}, u32[]{:S(2)}) async-start(bf16[4,32,128,128]{3,2,0,1:T(8,128)(2,1)} %select_bitcast_fusion.1), calls=%async_computation.1 | async-start | bytes 8388608 | tf_op jit(solution)/shard_map/all_to_all | solution.py:96
Sparse Core Ops, SparseCore 0:
  187.7 147.1 reduce-scatter.1
where the time goes:
time: 346 us; the launch traced here: 344 us
  matrix products  87.7 us (25%)
  waiting for transfers between devices  85.9 us (25%)
  other arithmetic  70.1 us (20%)
  local copies, waits for them, and re-layouts  68.4 us (20%)
  between operations  14.2 us (4%)
  blocking collectives  10.3 us (3%)
  starting transfers between devices  4.64 us (1%)
    all_to_all x1, waiting for transfers between devices, per_device(): lax.all_to_all(outgoing, ('group', 'dp'), split_axis=1, concat_axis=1, ti...  46.2 us
    reduce_sum x4, other arithmetic, attend(): jnp.sum(expo, axis=-1, keepdims=True)  40.7 us
    reduce_scatter x1, waiting for transfers between devices, per_device(): lax.psum_scatter(jnp.dot(attn, w_out, preferred_element_type=jnp.float32)...  39.7 us
    dot_general x4, matrix products, attend(): jnp.einsum('kgct,tkd->ckgd', weights, pairs[:, :, 1], preferred_element_t...  36.2 us
    dot_general x4, matrix products, attend(): jnp.einsum('ckgd,tkd->kgct', query_p, pairs[:, :, 0], preferred_element_t...  35.9 us
    unnamed x13, local copies, waits for them, and re-layouts  14.1 us
    all_gather x1, blocking collectives, per_device(): lengths_every = lax.all_gather(lengths, ('group', 'dp'), axis=0, tiled=True)  10.3 us
    select_n x4, other arithmetic, attend(): jnp.where(key_pos < window, (key_pos >= window - history) & (key_pos >= q...  8.15 us
  transfers between devices with their start and end apart: 2, of which 2 were waited for; matrix products, arithmetic and copies ran while one was open for 13% of the time, Pallas kernels for 0%

commit v1 on v0

--- a/solution.py
+++ b/solution.py
@@ -4,6 +4,18 @@
 from jax.sharding import PartitionSpec as P
 
 HD = 64
+
+
+def cut_along(shard, dim, devices):
+    shape = shard.shape
+    tiles = shard.reshape(*shape[:dim], devices, shape[dim] // devices, *shape[dim + 1 :])
+    return jnp.moveaxis(tiles, dim, 0)
+
+
+def laid_out(tiles, dim):
+    tiles = jnp.moveaxis(tiles, 0, dim)
+    lengths = tiles.shape
+    return tiles.reshape(*lengths[:dim], lengths[dim] * lengths[dim + 1], *lengths[dim + 2 :])
 
 
 def per_device(tokens, norm_gain, w_query, w_keyval, w_out, kv_cache, lengths, dest_slot):
@@ -93,7 +105,17 @@
     )
     raw_blocks = kv_cache.reshape(layers, per_dev, block_len, lane_width)
     outgoing = jnp.take(raw_blocks, send_idx, axis=1)
-    incoming = lax.all_to_all(outgoing, ("group", "dp"), split_axis=1, concat_axis=1, tiled=True)
+    size, index = (lax.axis_size(("group", "dp")), lax.axis_index(("group", "dp")))
+    blocks = cut_along(outgoing, 1, size)
+    out = blocks
+    for step in range(1, size):
+        target, source = ((index + step) % size, (index - step) % size)
+        sent = lax.dynamic_index_in_dim(blocks, target, 0)
+        received = lax.ppermute(
+            sent, ("group", "dp"), [(i, (i + step) % size) for i in range(size)]
+        )
+        out = lax.dynamic_update_slice_in_dim(out, received, source, axis=0)
+    incoming = laid_out(out, 1)
     where_from = senders * capacity + live_rank
     valid = (recv_all == my_index) & live_all
     slot_local = jnp.where(valid, dest_all - my_index * per_dev, per_dev)

time: 346 us -> 345 us (level)
  waiting for transfers between devices: 85.9 us -> 59.8 us
  local copies, waits for them, and re-layouts: 68.4 us -> 82.6 us
  starting transfers between devices: 4.64 us -> 14 us
    all_to_all x1 -> x0, waiting for transfers between devices: 46.2 us -> none  [per_device(): lax.all_to_all(outgoing, ('group', 'dp'), split_axis=1, concat_axis=1, ti...]
    ppermute x0 -> x7, waiting for transfers between devices: none -> 18.7 us  [per_device(): lax.ppermute(sent, ('group', 'dp'), [(i, (i + step) % size) for i in rang...]
    ppermute x0 -> x7, starting transfers between devices: none -> 13.9 us  [per_device(): lax.ppermute(sent, ('group', 'dp'), [(i, (i + step) % size) for i in rang...]
    dynamic_update_slice x0 -> x7, local copies, waits for them, and re-layouts: none -> 11.6 us  [per_device(): out = lax.dynamic_update_slice_in_dim(out, received, source, axis=0)]
    gather x1 -> x2, local copies, waits for them, and re-layouts: 6.48 us -> 11.2 us  [per_device(): outgoing = jnp.take(raw_blocks, send_idx, axis=1)]
    all_to_all x1 -> x0, local copies, waits for them, and re-layouts: 4.73 us -> none  [per_device(): lax.all_to_all(outgoing, ('group', 'dp'), split_axis=1, concat_axis=1, ti...]
    transpose x0 -> x1, other arithmetic: none -> 4.64 us  [cut_along(): return jnp.moveaxis(tiles, dim, 0)]
    all_to_all x1 -> x0, starting transfers between devices: 4.6 us -> none  [per_device(): lax.all_to_all(outgoing, ('group', 'dp'), split_axis=1, concat_axis=1, ti...]
  transfers between devices with their start and end apart: 2 -> 8, of which waited for: 2 -> 4; matrix products, arithmetic and copies ran while one was open for 13% -> 18% of each run, Pallas kernels for 0% -> 0%
where the time goes in v1:
time: 345 us; the launch traced here: 344 us
  matrix products  86.4 us (25%)
  local copies, waits for them, and re-layouts  82.6 us (24%)
  other arithmetic  72.9 us (21%)
  waiting for transfers between devices  59.8 us (17%)
  between operations  14.4 us (4%)
  starting transfers between devices  14 us (4%)
  blocking collectives  10.3 us (3%)
    reduce_scatter x1, waiting for transfers between devices, per_device(): lax.psum_scatter(jnp.dot(attn, w_out, preferred_element_type=jnp.float32)...  41.1 us
    reduce_sum x4, other arithmetic, attend(): jnp.sum(expo, axis=-1, keepdims=True)  40.7 us
    dot_general x4, matrix products, attend(): jnp.einsum('kgct,tkd->ckgd', weights, pairs[:, :, 1], preferred_element_t...  36.2 us
    dot_general x4, matrix products, attend(): jnp.einsum('ckgd,tkd->kgct', query_p, pairs[:, :, 0], preferred_element_t...  35.9 us
    ppermute x7, waiting for transfers between devices, per_device(): lax.ppermute(sent, ('group', 'dp'), [(i, (i + step) % size) for i in rang...  18.7 us
    unnamed x15, local copies, waits for them, and re-layouts  14.9 us
    ppermute x7, starting transfers between devices, per_device(): lax.ppermute(sent, ('group', 'dp'), [(i, (i + step) % size) for i in rang...  13.9 us
    dynamic_update_slice x7, local copies, waits for them, and re-layouts, per_device(): out = lax.dynamic_update_slice_in_dim(out, received, source, axis=0)  11.6 us
  transfers between devices with their start and end apart: 8, of which 4 were waited for; matrix products, arithmetic and copies ran while one was open for 18% of the time, Pallas kernels for 0%

profile of v1, /device:TPU:0, one launch (start us, length us, event | category | flops | bytes accessed | tf_op | source)
XLA Modules:
  0.0 343.6 jit_solution(7585218697769797410)
XLA Ops:
  26.8 5.2 %convolution_convert_fusion = bf16[1024,512]{1,0:T(8,128)(2,1)S(1)} fusion(bf16[2048,512]{1,0:T(8,128)(2,1)} %param.12, bf16[1024,2048]{1,0:T(8,128)(2,1)} %param.10, f32[2048]{0:T(1024)S(1)} %convert_element_type.40, f32[1024]{0:T(1024)S(1)} %add_rsqrt_fusion), kind=kOutput, calls=%fused_computation.49 | convolution fusion | flops 2156396544 | bytes 7352320 | tf_op jit(solution)/shard_map/dot_general | solution.py:39
  37.2 142.6 %while.14 = (s32[]{:T(128)}, bf16[4,256,512]{2,1,0:T(8,128)(2,1)}, s32[4]{0:T(128)}, bf16[4,2048,1,2,64]{1,4,3,2,0:T(8,128)(2,1)}, bf16[4,256,1,2,64]{1,4,3,2,0:...) while((s32[]{:T(128)}, bf16[4,256,512]{2,1,0:T(8,128)(2,1)}, ...), condition=%wide.region_4.5_spmd.clone.clone, body=%wide.region_1.4_spmd.clone.clone.sunk | while | flops 1268387072 | bytes 63510268 | solution.py:74
  42.4 9.0 %fusion.62 = (f32[8,256]{1,0:T(8,128)S(1)}, f32[2304,256,8]{1,0,2:T(8,128)}) fusion(pred[256,2304]{0,1:T(8,128)(4,1)S(1)} %fusion.61, bf16[4,256,1,8,64]{1,4,3,2,0:T(8,128)(2,1)} %get-tuple-element.308, s32[]{:T(128)S(6)} %copy.63, bf16[256,1,2,64]{0,3,2,1:T(8,128)(2,1)S(1)} %dynamic-slice_bitcast_fusion.11, ...), kind=kOutput, calls=%fused_computation.10.clone.1 | convolution fusion | flops 618723328 | bytes 20324356 | tf_op jit(solution)/shard_map/while/body/eval_jaxpr/ckgd,tkd->kgct/dot_general | solution.py:52
  51.4 10.2 %fusion.63 = f32[8,256]{1,0:T(8,128)S(1)} fusion(f32[2304,256,8]{1,0,2:T(8,128)} %get-tuple-element.282, f32[8,256]{1,0:T(8,128)S(1)} %get-tuple-element.283, pred[256,2304]{0,1:T(8,128)(4,1)S(1)} %fusion.61), kind=kLoop, calls=%fused_computation.9.clone.1 | loop fusion | flops 18872320 | bytes 19480576 | tf_op jit(solution)/shard_map/while/body/eval_jaxpr/reduce_sum | solution.py:65
  61.6 9.0 %fusion.64 = bf16[64,8,256]{2,0,1:T(8,128)(2,1)S(1)} fusion(f32[8,256]{1,0:T(8,128)S(1)} %fusion.63, f32[8,256]{1,0:T(8,128)S(1)} %get-tuple-element.283, f32[2304,256,8]{1,0,2:T(8,128)} %get-tuple-element.282, pred[256,2304]{0,1:T(8,128)(4,1)S(1)} %fusion.61, bf16[2048,1,2,64]{0,3,2,1:T(8,128)(2,1)S(1)} %dynamic-slice_bitcast_fusion.12, ...), kind=kOutput, calls=%fused_computation.17.clone.1 | convolution fusion | flops 628293632 | bytes 20332544 | tf_op jit(solution)/shard_map/while/body/eval_jaxpr/kgct,tkd->ckgd/dot_general | solution.py:66
  78.0 9.0 %fusion.62 = (f32[8,256]{1,0:T(8,128)S(1)}, f32[2304,256,8]{1,0,2:T(8,128)}) fusion(pred[256,2304]{0,1:T(8,128)(4,1)S(1)} %fusion.61, bf16[4,256,1,8,64]{1,4,3,2,0:T(8,128)(2,1)} %get-tuple-element.308, s32[]{:T(128)S(6)} %copy.63, bf16[256,1,2,64]{0,3,2,1:T(8,128)(2,1)S(1)} %dynamic-slice_bitcast_fusion.11, ...), kind=kOutput, calls=%fused_computation.10.clone.1 | convolution fusion | flops 618723328 | bytes 20324356 | tf_op jit(solution)/shard_map/while/body/eval_jaxpr/ckgd,tkd->kgct/dot_general | solution.py:52
  87.0 10.2 %fusion.63 = f32[8,256]{1,0:T(8,128)S(1)} fusion(f32[2304,256,8]{1,0,2:T(8,128)} %get-tuple-element.282, f32[8,256]{1,0:T(8,128)S(1)} %get-tuple-element.283, pred[256,2304]{0,1:T(8,128)(4,1)S(1)} %fusion.61), kind=kLoop, calls=%fused_computation.9.clone.1 | loop fusion | flops 18872320 | bytes 19480576 | tf_op jit(solution)/shard_map/while/body/eval_jaxpr/reduce_sum | solution.py:65
  97.2 9.0 %fusion.64 = bf16[64,8,256]{2,0,1:T(8,128)(2,1)S(1)} fusion(f32[8,256]{1,0:T(8,128)S(1)} %fusion.63, f32[8,256]{1,0:T(8,128)S(1)} %get-tuple-element.283, f32[2304,256,8]{1,0,2:T(8,128)} %get-tuple-element.282, pred[256,2304]{0,1:T(8,128)(4,1)S(1)} %fusion.61, bf16[2048,1,2,64]{0,3,2,1:T(8,128)(2,1)S(1)} %dynamic-slice_bitcast_fusion.12, ...), kind=kOutput, calls=%fused_computation.17.clone.1 | convolution fusion | flops 628293632 | bytes 20332544 | tf_op jit(solution)/shard_map/while/body/eval_jaxpr/kgct,tkd->ckgd/dot_general | solution.py:66
  113.7 9.0 %fusion.62 = (f32[8,256]{1,0:T(8,128)S(1)}, f32[2304,256,8]{1,0,2:T(8,128)}) fusion(pred[256,2304]{0,1:T(8,128)(4,1)S(1)} %fusion.61, bf16[4,256,1,8,64]{1,4,3,2,0:T(8,128)(2,1)} %get-tuple-element.308, s32[]{:T(128)S(6)} %copy.63, bf16[256,1,2,64]{0,3,2,1:T(8,128)(2,1)S(1)} %dynamic-slice_bitcast_fusion.11, ...), kind=kOutput, calls=%fused_computation.10.clone.1 | convolution fusion | flops 618723328 | bytes 20324356 | tf_op jit(solution)/shard_map/while/body/eval_jaxpr/ckgd,tkd->kgct/dot_general | solution.py:52
  122.7 10.2 %fusion.63 = f32[8,256]{1,0:T(8,128)S(1)} fusion(f32[2304,256,8]{1,0,2:T(8,128)} %get-tuple-element.282, f32[8,256]{1,0:T(8,128)S(1)} %get-tuple-element.283, pred[256,2304]{0,1:T(8,128)(4,1)S(1)} %fusion.61), kind=kLoop, calls=%fused_computation.9.clone.1 | loop fusion | flops 18872320 | bytes 19480576 | tf_op jit(solution)/shard_map/while/body/eval_jaxpr/reduce_sum | solution.py:65
  132.9 9.0 %fusion.64 = bf16[64,8,256]{2,0,1:T(8,128)(2,1)S(1)} fusion(f32[8,256]{1,0:T(8,128)S(1)} %fusion.63, f32[8,256]{1,0:T(8,128)S(1)} %get-tuple-element.283, f32[2304,256,8]{1,0,2:T(8,128)} %get-tuple-element.282, pred[256,2304]{0,1:T(8,128)(4,1)S(1)} %fusion.61, bf16[2048,1,2,64]{0,3,2,1:T(8,128)(2,1)S(1)} %dynamic-slice_bitcast_fusion.12, ...), kind=kOutput, calls=%fused_computation.17.clone.1 | convolution fusion | flops 628293632 | bytes 20332544 | tf_op jit(solution)/shard_map/while/body/eval_jaxpr/kgct,tkd->ckgd/dot_general | solution.py:66
  149.3 9.0 %fusion.62 = (f32[8,256]{1,0:T(8,128)S(1)}, f32[2304,256,8]{1,0,2:T(8,128)}) fusion(pred[256,2304]{0,1:T(8,128)(4,1)S(1)} %fusion.61, bf16[4,256,1,8,64]{1,4,3,2,0:T(8,128)(2,1)} %get-tuple-element.308, s32[]{:T(128)S(6)} %copy.63, bf16[256,1,2,64]{0,3,2,1:T(8,128)(2,1)S(1)} %dynamic-slice_bitcast_fusion.11, ...), kind=kOutput, calls=%fused_computation.10.clone.1 | convolution fusion | flops 618723328 | bytes 20324356 | tf_op jit(solution)/shard_map/while/body/eval_jaxpr/ckgd,tkd->kgct/dot_general | solution.py:52
  158.3 10.2 %fusion.63 = f32[8,256]{1,0:T(8,128)S(1)} fusion(f32[2304,256,8]{1,0,2:T(8,128)} %get-tuple-element.282, f32[8,256]{1,0:T(8,128)S(1)} %get-tuple-element.283, pred[256,2304]{0,1:T(8,128)(4,1)S(1)} %fusion.61), kind=kLoop, calls=%fused_computation.9.clone.1 | loop fusion | flops 18872320 | bytes 19480576 | tf_op jit(solution)/shard_map/while/body/eval_jaxpr/reduce_sum | solution.py:65
  168.5 9.0 %fusion.64 = bf16[64,8,256]{2,0,1:T(8,128)(2,1)S(1)} fusion(f32[8,256]{1,0:T(8,128)S(1)} %fusion.63, f32[8,256]{1,0:T(8,128)S(1)} %get-tuple-element.283, f32[2304,256,8]{1,0,2:T(8,128)} %get-tuple-element.282, pred[256,2304]{0,1:T(8,128)(4,1)S(1)} %fusion.61, bf16[2048,1,2,64]{0,3,2,1:T(8,128)(2,1)S(1)} %dynamic-slice_bitcast_fusion.12, ...), kind=kOutput, calls=%fused_computation.17.clone.1 | convolution fusion | flops 628293632 | bytes 20332544 | tf_op jit(solution)/shard_map/while/body/eval_jaxpr/kgct,tkd->ckgd/dot_general | solution.py:66
  179.9 6.8 %fusion.47 = f32[1024,2048]{1,0:T(8,128)} fusion(bf16[1024,512]{1,0:T(8,128)(2,1)} %bitcast.129, bf16[512,2048]{1,0:T(8,128)(2,1)S(1)} %copy-done), kind=kOutput, calls=%fused_computation.108 | convolution fusion | flops 2147483648 | bytes 11534336 | tf_op jit(solution)/shard_map/dot_general | solution.py:77
  187.5 10.3 %all-gather = s32[8,4,2]{1,2,0:T(2,128)S(1)} all-gather(s32[1,4,2]{1,2,0:T(2,128)S(1)} %bitcast.127), channel_id=1, replica_groups=mesh['group'=4,'dp'=2,'tensor'=4] {'group','dp'}, dimensions={0}, use_global_device_ids=true | all-gather | bytes 288 | tf_op jit(solution)/shard_map/all_gather | solution.py:93
  199.7 6.5 %gather_fusion = bf16[32,4,128,128]{3,2,1,0:T(8,128)(2,1)} fusion(bf16[4,64,128,128]{3,2,1,0:T(8,128)(2,1)} %bitcast.126, s32[1024]{0:T(1024)S(1)} %pad_clamp_fusion.1), kind=kCustom, calls=%fused_computation | custom fusion | bytes 8388736 | tf_op jit(solution)/shard_map/jit(_take)/gather | solution.py:107
  232.4 9.0 %collective-permute-start.6 = (bf16[1,4,4,128,128]{4,3,2,0,1:T(8,128)(2,1)S(1)}, bf16[1,4,4,128,128]{4,3,2,0,1:T(8,128)(2,1)S(1)}, u32[]{:S(2)}, u32[]{:S(2)}) collective-permute-start(bf16[1,4,4,128,128]{4,3,2,0,1:T(8,128)(2,1)S(1)} %get-tuple-element.224), channel_id=1, source_target_pairs={{0,28},{4,0},{8,4},{12,8},{16,12},{20,16},{24,20},{28,24},{1,29},{... | collective-permute-start | bytes 1572872 | tf_op jit(solution)/shard_map/ppermute | solution.py:114
  243.4 9.7 %collective-permute-done.2 = bf16[1,4,4,128,128]{4,3,2,0,1:T(8,128)(2,1)} collective-permute-done((bf16[1,4,4,128,128]{4,3,2,0,1:T(8,128)(2,1)}, bf16[1,4,4,128,128]{4,3,2,0,1:T(8,128)(2,1)}, u32[]{:S(2)}, u32[]{:S(2)}) %collective-permute-start.2) | collective-permute-done | bytes 524320 | tf_op jit(solution)/shard_map/ppermute | solution.py:114
  257.0 6.4 %collective-permute-done.4 = bf16[1,4,4,128,128]{4,3,2,0,1:T(8,128)(2,1)} collective-permute-done((bf16[1,4,4,128,128]{4,3,2,0,1:T(8,128)(2,1)}, bf16[1,4,4,128,128]{4,3,2,0,1:T(8,128)(2,1)}, u32[]{:S(2)}, u32[]{:S(2)}) %collective-permute-start.4) | collective-permute-done | bytes 524320 | tf_op jit(solution)/shard_map/ppermute | solution.py:114
  267.2 7.8 %gather_fusion.1 = bf16[64,4,128,128]{3,2,1,0:T(8,128)(2,1)} fusion(bf16[4,32,128,128]{3,2,1,0:T(8,128)(2,1)} %bitcast.122, s32[1024]{0:T(1024)S(1)} %pad_clamp_fusion), kind=kCustom, calls=%fused_computation.1 | custom fusion | bytes 16777472 | tf_op jit(solution)/shard_map/jit(_take)/gather | solution.py:127
  275.0 7.3 %select_bitcast_fusion = bf16[4,64,128,128]{3,2,0,1:T(8,128)(2,1)} fusion(bf16[64,4,128,128]{3,2,1,0:T(8,128)(2,1)} %gather_fusion.1, pred[64]{0:T(512)(128)(4,1)S(1)} %compare_and_fusion.1), kind=kLoop, calls=%fused_computation.47 | loop fusion | flops 4194304 | bytes 16777280 | tf_op jit(solution)/shard_map/jit(_take)/select_n | solution.py:127
  282.3 10.6 %copy.50 = bf16[4,64,128,128]{3,2,1,0:T(8,128)(2,1)} copy(bf16[4,64,128,128]{3,2,0,1:T(8,128)(2,1)} %select_bitcast_fusion) | data formatting | bytes 16777216
  292.9 41.1 %reduce-scatter.2.cloned.1.call-done = f32[256,2048]{1,0:T(8,128)} async-done(((f32[1024,2048]{1,0:T(8,128)}), f32[256,2048]{1,0:T(8,128)}) %reduce-scatter.2.cloned.1.call-update) | async-done | bytes 2097168 | tf_op jit(solution)/shard_map/reduce_scatter | solution.py:76
  (138 shorter events, 92.5 us)
Async XLA Ops:
  7.2 172.7 %copy-start = (bf16[512,2048]{1,0:T(8,128)(2,1)S(1)}, bf16[512,2048]{1,0:T(8,128)(2,1)}, u32[]{:S(2)}) copy-start(bf16[512,2048]{1,0:T(8,128)(2,1)} %param.14) | copy-start | bytes 6291460
  7.2 326.8 %reduce-scatter.2.cloned.1.call-start = ((), (), s32[]{:S(2)}) async-start(), calls=%async_computation.1 | async-start | bytes 10485760 | tf_op jit(solution)/shard_map/reduce_scatter | solution.py:76
  11.7 8.7 %copy-start.3 = (bf16[2048]{0:T(1024)(128)(2,1)S(1)}, bf16[2048]{0:T(1024)(128)(2,1)}, u32[]{:S(2)}) copy-start(bf16[2048]{0:T(1024)(128)(2,1)} %param.11) | copy-start | bytes 12292
  20.4 3.4 %copy-start.1 = (bf16[1024,2048]{1,0:T(8,128)(2,1)S(1)}, bf16[1024,2048]{1,0:T(8,128)(2,1)}, u32[]{:S(2)}) copy-start(bf16[1024,2048]{1,0:T(8,128)(2,1)} %param.10) | copy-start | bytes 12582916
  61.5 9.1 %copy-start.5 = (s32[4]{0:T(128)S(1)}, s32[4]{0:T(128)}, u32[]{:S(2)}) copy-start(s32[4]{0:T(128)} %get-tuple-element.304) | copy-start | bytes 52 | tf_op jit(solution)/shard_map/while
  97.2 9.1 %copy-start.5 = (s32[4]{0:T(128)S(1)}, s32[4]{0:T(128)}, u32[]{:S(2)}) copy-start(s32[4]{0:T(128)} %get-tuple-element.304) | copy-start | bytes 52 | tf_op jit(solution)/shard_map/while
  132.8 9.1 %copy-start.5 = (s32[4]{0:T(128)S(1)}, s32[4]{0:T(128)}, u32[]{:S(2)}) copy-start(s32[4]{0:T(128)} %get-tuple-element.304) | copy-start | bytes 52 | tf_op jit(solution)/shard_map/while
  168.5 9.1 %copy-start.5 = (s32[4]{0:T(128)S(1)}, s32[4]{0:T(128)}, u32[]{:S(2)}) copy-start(s32[4]{0:T(128)} %get-tuple-element.304) | copy-start | bytes 52 | tf_op jit(solution)/shard_map/while
  186.7 0.7 copy-start.2
  186.7 0.8 copy-start.4
  215.3 14.7 %collective-permute-start = (bf16[1,4,4,128,128]{4,3,2,0,1:T(8,128)(2,1)}, bf16[1,4,4,128,128]{4,3,2,0,1:T(8,128)(2,1)}, u32[]{:S(2)}, u32[]{:S(2)}) collective-permute-start(bf16[1,4,4,128,128]{4,3,2,0,1:T(8,128)(2,1)} %get-tuple-element.230), channel_id=1, source_target_pairs={{0,4},{4,8},{8,12},{12,16},{16,20},{20,24},{24,28},{28,0},{1,5},{5... | collective-permute-start | bytes 1572872 | tf_op jit(solution)/shard_map/ppermute | solution.py:114
  215.6 16.9 %collective-permute-start.1 = (bf16[1,4,4,128,128]{4,3,2,0,1:T(8,128)(2,1)}, bf16[1,4,4,128,128]{4,3,2,0,1:T(8,128)(2,1)}, u32[]{:S(2)}, u32[]{:S(2)}) collective-permute-start(bf16[1,4,4,128,128]{4,3,2,0,1:T(8,128)(2,1)} %get-tuple-element.229), channel_id=1, source_target_pairs={{0,8},{4,12},{8,16},{12,20},{16,24},{20,28},{24,0},{28,4},{1,9},{5... | collective-permute-start | bytes 1572872 | tf_op jit(solution)/shard_map/ppermute | solution.py:114
  217.1 36.0 %collective-permute-start.2 = (bf16[1,4,4,128,128]{4,3,2,0,1:T(8,128)(2,1)}, bf16[1,4,4,128,128]{4,3,2,0,1:T(8,128)(2,1)}, u32[]{:S(2)}, u32[]{:S(2)}) collective-permute-start(bf16[1,4,4,128,128]{4,3,2,0,1:T(8,128)(2,1)} %get-tuple-element.228), channel_id=1, source_target_pairs={{0,12},{4,16},{8,20},{12,24},{16,28},{20,0},{24,4},{28,8},{1,13},{... | collective-permute-start | bytes 1572872 | tf_op jit(solution)/shard_map/ppermute | solution.py:114
  218.2 36.8 %collective-permute-start.3 = (bf16[1,4,4,128,128]{4,3,2,0,1:T(8,128)(2,1)}, bf16[1,4,4,128,128]{4,3,2,0,1:T(8,128)(2,1)}, u32[]{:S(2)}, u32[]{:S(2)}) collective-permute-start(bf16[1,4,4,128,128]{4,3,2,0,1:T(8,128)(2,1)} %get-tuple-element.227), channel_id=1, source_target_pairs={{0,16},{4,20},{8,24},{12,28},{16,0},{20,4},{24,8},{28,12},{1,17},{... | collective-permute-start | bytes 1572872 | tf_op jit(solution)/shard_map/ppermute | solution.py:114
  219.7 43.7 %collective-permute-start.4 = (bf16[1,4,4,128,128]{4,3,2,0,1:T(8,128)(2,1)}, bf16[1,4,4,128,128]{4,3,2,0,1:T(8,128)(2,1)}, u32[]{:S(2)}, u32[]{:S(2)}) collective-permute-start(bf16[1,4,4,128,128]{4,3,2,0,1:T(8,128)(2,1)} %get-tuple-element.226), channel_id=1, source_target_pairs={{0,20},{4,24},{8,28},{12,0},{16,4},{20,8},{24,12},{28,16},{1,21},{... | collective-permute-start | bytes 1572872 | tf_op jit(solution)/shard_map/ppermute | solution.py:114
  229.9 35.5 %collective-permute-start.5 = (bf16[1,4,4,128,128]{4,3,2,0,1:T(8,128)(2,1)S(1)}, bf16[1,4,4,128,128]{4,3,2,0,1:T(8,128)(2,1)S(1)}, u32[]{:S(2)}, u32[]{:S(2)}) collective-permute-start(bf16[1,4,4,128,128]{4,3,2,0,1:T(8,128)(2,1)S(1)} %get-tuple-element.225), channel_id=1, source_target_pairs={{0,24},{4,28},{8,0},{12,4},{16,8},{20,12},{24,16},{28,20},{1,25},{... | collective-permute-start | bytes 1572872 | tf_op jit(solution)/shard_map/ppermute | solution.py:114
  232.4 33.8 %collective-permute-start.6 = (bf16[1,4,4,128,128]{4,3,2,0,1:T(8,128)(2,1)S(1)}, bf16[1,4,4,128,128]{4,3,2,0,1:T(8,128)(2,1)S(1)}, u32[]{:S(2)}, u32[]{:S(2)}) collective-permute-start(bf16[1,4,4,128,128]{4,3,2,0,1:T(8,128)(2,1)S(1)} %get-tuple-element.224), channel_id=1, source_target_pairs={{0,28},{4,0},{8,4},{12,8},{16,12},{20,16},{24,20},{28,24},{1,29},{... | collective-permute-start | bytes 1572872 | tf_op jit(solution)/shard_map/ppermute | solution.py:114
Sparse Core Ops, SparseCore 0:
  186.8 147.1 reduce-scatter.1
